TPU v7x, 256 devices: a whole 4x4x8 slice. The times are simulated.
256 devices in a mesh: depth: 16 (over x, y), tile: 16 (over z, core).
Axes of the slice: x: 4, y: 4, z: 8, core: 2. Of those that a mesh axis runs over, the one named last changes fastest.
Arguments:
- density: float32 [512, 512, 2048], P('depth', 'tile'), may hold values from 0 to 1
- palette: float32 [2, 3], replicated, may hold values from 0.2 to 1
- light_dir: float32 [2, 3], replicated, may hold values from -4 to 4
- slab_of: int32 [16], replicated, may hold values from 0 to 15, each once
Outputs:
- images: float32 [2, 4, 512, 2048], P(None, None, 'tile', 'depth')
Inputs may be any that keep to these rules, and one draw needn't show every extreme that they name: `slab_of`: each of 0 to 15 appears once.
All inputs are finite; a program needn't handle non-finite values.
Results may differ from a plain program's by a relative error of at most 0.0008.
Values may be sent and summed in bfloat16 or wider, within the bound.
No kernel may reach another device: no remote copies, remote signals or barrier semaphores. Data moves between devices by JAX's collectives and lax.ppermute only.
A program may use at most 128 MiB of HBM per device.

v0:
```python
import jax
import jax.numpy as jnp
from jax import lax
from jax.sharding import PartitionSpec as P

HIGH = lax.Precision.HIGHEST


def padded_2(block, sides, width):
    for axis, dim in sides:
        count = lax.axis_size(axis)
        forward = [(i, i + 1) for i in range(count - 1)]
        backward = [(target, source) for source, target in forward]
        low = lax.ppermute(
            lax.slice_in_dim(block, block.shape[dim] - width, None, axis=dim), axis, forward
        )
        high = lax.ppermute(lax.slice_in_dim(block, 0, width, axis=dim), axis, backward)
        block = jnp.concatenate([low, block, high], axis=dim)
    return block


def centred(field, axis):
    size = field.shape[axis]
    upper = jnp.concatenate(
        [
            lax.slice_in_dim(field, 1, size, axis=axis),
            lax.slice_in_dim(field, size - 1, size, axis=axis),
        ],
        axis,
    )
    lower = jnp.concatenate(
        [lax.slice_in_dim(field, 0, 1, axis=axis), lax.slice_in_dim(field, 0, size - 1, axis=axis)],
        axis,
    )
    return (upper - lower) * 0.5


def march(block, grad_x, palette, light_dir, factor):
    grad_z = centred(block, 0)
    grad_y = centred(block, 2)
    length = jnp.sqrt(grad_x * grad_x + grad_y * grad_y + grad_z * grad_z + 0.25)
    optical = block * factor
    opacity = 1.0 - jnp.exp(-optical)
    running = jnp.cumsum(optical, axis=0)
    slab_tau = running[-1]
    before = [running - optical, slab_tau[None] - running]
    colours = []
    for view in range(2):
        facing = (
            grad_x * light_dir[view, 0] + grad_y * light_dir[view, 1] + grad_z * light_dir[view, 2]
        )
        shade = 0.3 + jnp.abs(facing) / length
        weight = opacity * jnp.exp(-before[view]) * shade
        plain = jnp.sum(weight, axis=0)
        dense = jnp.sum(block * weight, axis=0)
        colours.append(
            palette[0][:, None, None] * plain[None] + palette[1][:, None, None] * dense[None]
        )
    return (jnp.stack(colours).astype(jnp.bfloat16), slab_tau.astype(jnp.bfloat16))


def on_device(density, palette, light_dir, slab_of):
    slab_rows, tile_rows, image_cols = density.shape
    depth_count = lax.axis_size("depth")
    tile_count = lax.axis_size("tile")
    tile_place = lax.axis_index("tile")
    depth_place = lax.axis_index("depth")
    padded = padded_2(density, (("tile", 1),), 1)
    left_plane = jnp.where(tile_place == 0, density[:, :1], padded[:, :1])
    right_plane = jnp.where(tile_place == tile_count - 1, density[:, -1:], padded[:, -1:])
    full_x = jnp.concatenate([left_plane, density, right_plane], axis=1)
    grad_x = (full_x[:, 2:] - full_x[:, :-2]) * 0.5
    factor = 3.0 / (slab_rows * depth_count)
    slab_rgb, slab_tau = march(density, grad_x, palette, light_dir, factor)
    piece_width = image_cols // depth_count
    my_slab = slab_of[depth_place]
    earlier = (slab_of < my_slab).astype(jnp.float32)
    later = (slab_of > my_slab).astype(jnp.float32)
    tau_full = lax.all_gather(slab_tau[None], "depth", axis=0, tiled=True).astype(jnp.float32)
    front_one = jnp.einsum("k,kxy->xy", earlier, tau_full, precision=HIGH)
    front_two = jnp.einsum("k,kxy->xy", later, tau_full, precision=HIGH)
    total = jnp.sum(tau_full, axis=0)
    fading = jnp.exp(-jnp.stack([front_one, front_two]))
    terms = slab_rgb.astype(jnp.float32) * fading[:, None]
    colours = lax.psum_scatter(terms, "depth", scatter_dimension=3, tiled=True)
    coverage = lax.dynamic_slice_in_dim(
        1.0 - jnp.exp(-total), depth_place * piece_width, piece_width, 1
    )
    coverage = jnp.broadcast_to(coverage[None, None], (2, 1, tile_rows, piece_width))
    return jnp.concatenate([colours, coverage], axis=1)


def solution(mesh):
    in_specs = (P("depth", "tile", None), P(), P(), P())
    out_specs = P(None, None, "tile", "depth")
    return jax.shard_map(
        on_device, mesh=mesh, in_specs=in_specs, out_specs=out_specs, check_vma=False
    )
```

profile of v0, /device:TPU:2, one launch (start us, length us, event | category | flops | bytes accessed | tf_op | source)
XLA Modules:
  0.0 228.3 jit_solution(13227945402182114814)
XLA Ops:
  6.5 2.7 %fusion.23 = (f32[32,1,2048]{2,1,0:T(1,128)S(1)}, f32[32,1,2048]{2,1,0:T(1,128)S(1)}) fusion(f32[32,32,2048]{2,1,0:T(8,128)} %param.4), kind=kLoop, calls=%fused_computation.46 | loop fusion | bytes 1048576 | tf_op jit(solution)/shard_map/slice | solution.py:69
  9.2 1.3 collective-permute-start
  10.5 3.0 %collective-permute-start.1 = (f32[32,1,2048]{2,1,0:T(1,128)S(1)}, f32[32,1,2048]{2,1,0:T(1,128)S(1)}, u32[]{:S(2)}, u32[]{:S(2)}) collective-permute-start(f32[32,1,2048]{2,1,0:T(1,128)S(1)} %get-tuple-element.20), channel_id=1, source_target_pairs={{0,1},{1,2},{2,3},{3,4},{4,5},{5,6},{6,7},{7,8},{8,9},{9,10},{10,1... | collective-permute-start | bytes 786440 | tf_op jit(solution)/shard_map/ppermute | solution.py:14
  13.6 1.2 fusion.22
  14.8 11.5 %fusion.21 = (f32[31,32,2048]{2,1,0:T(8,128)}, f32[31,32,2048]{2,1,0:T(8,128)}) fusion(f32[32,32,2048]{2,1,0:T(8,128)} %param.4), kind=kLoop, calls=%fused_computation.44 | loop fusion | bytes 32505856 | tf_op jit(solution)/shard_map/slice | solution.py:26
  26.4 7.3 %fusion.19 = (f32[32,32,2047]{2,1,0:T(8,128)}, f32[32,32,2047]{2,1,0:T(8,128)}) fusion(f32[32,32,2048]{2,1,0:T(8,128)S(1)} %bitcast.22), kind=kLoop, calls=%fused_computation.42 | loop fusion | bytes 33538048 | tf_op jit(solution)/shard_map/slice | solution.py:26
  33.7 0.7 fusion.24
  38.1 0.7 dynamic_slice.6
  38.8 1.4 fusion.20
  40.2 2.9 %broadcast_select_fusion.1 = (f32[32,1,2048]{2,1,0:T(1,128)S(1)}, f32[32,1,2048]{2,1,0:T(1,128)S(1)}) fusion(f32[32,1,2048]{2,1,0:T(1,128)S(1)} %collective-permute-done, pred[]{:T(512)S(6)} %eq.6, f32[32,32,2048]{2,1,0:T(8,128)} %param.4, f32[32,1,2048]{2,1,0:T(1,128)S(1)} %collective-permute-done.1, pred[]{:T(512)S(6)} %eq.7), kind=kLoop, calls=%fused_computation.25 | loop fusion | flops 131072 | bytes 1572866 | tf_op jit(solution)/shard_map/jit(_where)/select_n | solution.py:70
  43.1 30.5 %add_multiply_fusion.1 = (f32[32,32,2048]{2,1,0:T(8,128)}, f32[32,32,2048]{2,1,0:T(8,128)}) fusion(f32[32,32,2048]{2,1,0:T(8,128)} %param.4, f32[32,1,2048]{2,1,0:T(1,128)S(1)} %get-tuple-element.18, f32[32,1,2048]{2,1,0:T(1,128)S(1)} %get-tuple-element.17, f32[]{:T(128)} %bitcast.3, f32[]{:T(128)} %bitcast.2, f32[]{:T(128)} %bitcast.1, ...), kind=kOutput, calls=%fused_computation.8 | output fusion | flops 136314880 | bytes 59244556 | tf_op jit(solution)/shard_map/jit(cumsum)/reduce_window_sum | solution.py:44
  73.6 1.6 slice.97
  75.2 1.0 slice_bitcast_fusion
  76.2 0.2 reduce-scatter.2.cloned.1.call-start
  76.5 31.7 %fusion.18 = (f32[32,2048]{1,0:T(8,128)S(1)}, f32[32,2048]{1,0:T(8,128)S(1)}, f32[32,2048]{1,0:T(8,128)S(1)}, f32[32,2048]{1,0:T(8,128)S(1)}) fusion(f32[32,32,2048]{2,1,0:T(8,128)} %get-tuple-element.31, f32[32,32,2048]{2,1,0:T(8,128)} %param.4, f32[]{:T(128)} %bitcast.8, f32[31,32,2048]{2,1,0:T(8,128)} %get-tuple-element.14, ...), kind=kLoop, calls=%fused_computation.41 | loop fusion | flops 81526784 | bytes 60555276 | tf_op jit(solution)/shard_map/reduce_sum | solution.py:54
  108.2 0.3 add_convert_fusion.1
  108.5 21.2 %all-gather.2.cloned.1.call-done = bf16[16,32,2048]{2,1,0:T(8,128)(2,1)} async-done(((bf16[1,32,2048]{2,1,0:T(8,128)(2,1)}), bf16[16,32,2048]{2,1,0:T(8,128)(2,1)}) %all-gather.2.cloned.1.call-update) | async-done | bytes 2097168 | tf_op jit(solution)/shard_map/all_gather | solution.py:79
  129.6 4.8 %fusion.4 = f32[1,32,2048]{2,0,1:T(1,128)S(1)} fusion(bf16[16,32,2048]{2,1,0:T(8,128)(2,1)} %all-gather.2.cloned.1.call-done, s32[16]{0:T(128)S(1)} %copy-done.2, s32[]{:T(128)} %bitcast.9), kind=kOutput, calls=%fused_computation.15 | convolution fusion | flops 2097168 | bytes 2359364 | tf_op jit(solution)/shard_map/k,kxy->xy/dot_general | solution.py:81
  134.5 0.1 copy.7
  134.5 4.7 %fusion.6 = f32[1,32,2048]{2,0,1:T(1,128)S(1)} fusion(bf16[16,32,2048]{2,1,0:T(8,128)(2,1)} %all-gather.2.cloned.1.call-done, s32[16]{0:T(128)S(1)} %copy-done.2, s32[]{:T(128)} %bitcast.9), kind=kOutput, calls=%fused_computation.17 | convolution fusion | flops 2097168 | bytes 2359364 | tf_op jit(solution)/shard_map/k,kxy->xy/dot_general | solution.py:80
  139.4 1.3 convert_multiply_fusion
  140.7 0.4 convert_reduce_fusion
  141.1 78.8 %reduce-scatter.2.cloned.1.call-done = f32[2,3,32,128]{3,2,1,0:T(8,128)} async-done(((f32[2,3,32,2048]{3,2,1,0:T(8,128)}), f32[2,3,32,128]{3,2,1,0:T(8,128)}) %reduce-scatter.2.cloned.1.call-update) | async-done | bytes 98320 | tf_op jit(solution)/shard_map/reduce_scatter | solution.py:85
  219.9 1.6 pad_maximum_fusion.2
  (23 shorter events, 0.3 us)
Async XLA Ops:
  6.5 123.1 %all-gather.2.cloned.1.call-start = ((), (), s32[]{:S(2)}) async-start(), calls=%async_computation.1 | async-start | bytes 2228224 | tf_op jit(solution)/shard_map/all_gather | solution.py:79
  9.2 31.0 %collective-permute-start = (f32[32,1,2048]{2,1,0:T(1,128)S(1)}, f32[32,1,2048]{2,1,0:T(1,128)S(1)}, u32[]{:S(2)}, u32[]{:S(2)}) collective-permute-start(f32[32,1,2048]{2,1,0:T(1,128)S(1)} %get-tuple-element.19), channel_id=1, source_target_pairs={{1,0},{2,1},{3,2},{4,3},{5,4},{6,5},{7,6},{8,7},{9,8},{10,9},{11,1... | collective-permute-start | bytes 786440 | tf_op jit(solution)/shard_map/ppermute | solution.py:17
  10.5 29.7 %collective-permute-start.1 = (f32[32,1,2048]{2,1,0:T(1,128)S(1)}, f32[32,1,2048]{2,1,0:T(1,128)S(1)}, u32[]{:S(2)}, u32[]{:S(2)}) collective-permute-start(f32[32,1,2048]{2,1,0:T(1,128)S(1)} %get-tuple-element.20), channel_id=1, source_target_pairs={{0,1},{1,2},{2,3},{3,4},{4,5},{5,6},{6,7},{7,8},{8,9},{9,10},{10,1... | collective-permute-start | bytes 786440 | tf_op jit(solution)/shard_map/ppermute | solution.py:14
  13.6 12.8 %slice-start = ((s8[8388608]{0:T(1024)(128)(4,1)}), s8[4194304]{0:T(1024)(128)(4,1)S(1)}, s32[]{:S(2)}) async-start(s8[8388608]{0:T(1024)(128)(4,1)} %bitcast.21), calls=%async_computation.3 | async-start | bytes 8388608
  14.8 11.5 %slice-start.1 = ((s8[8388608]{0:T(1024)(128)(4,1)}), s8[4194304]{0:T(1024)(128)(4,1)S(1)}, s32[]{:S(2)}) async-start(s8[8388608]{0:T(1024)(128)(4,1)} %bitcast.21), calls=%async_computation.4 | async-start | bytes 8388608
  26.3 7.3 %copy-start.3 = (f32[2,3]{1,0:T(2,128)S(1)}, f32[2,3]{1,0:T(2,128)}, u32[]{:S(2)}) copy-start(f32[2,3]{1,0:T(2,128)} %param.5) | copy-start | bytes 76
  26.3 7.3 %copy-start.1 = (f32[2,3]{1,0:T(2,128)S(1)}, f32[2,3]{1,0:T(2,128)}, u32[]{:S(2)}) copy-start(f32[2,3]{1,0:T(2,128)} %param.6) | copy-start | bytes 76
  26.4 11.8 %copy-start.2 = (s32[16]{0:T(128)S(1)}, s32[16]{0:T(128)}, u32[]{:S(2)}) copy-start(s32[16]{0:T(128)} %param.7) | copy-start | bytes 196
  76.2 143.6 %reduce-scatter.2.cloned.1.call-start = ((), (), s32[]{:S(2)}) async-start(), calls=%async_computation.2 | async-start | bytes 1671168 | tf_op jit(solution)/shard_map/reduce_scatter | solution.py:85
  129.6 11.1 %copy-start = (bf16[16,32,2048]{2,1,0:T(8,128)(2,1)S(1)}, bf16[16,32,2048]{2,1,0:T(8,128)(2,1)}, u32[]{:S(2)}) copy-start(bf16[16,32,2048]{2,1,0:T(8,128)(2,1)} %all-gather.2.cloned.1.call-done) | copy-start | bytes 6291460
Sparse Core Ops, SparseCore 0:
  76.4 53.2 all-gather.1
  140.8 79.0 reduce-scatter.1
where the time goes:
time: 229 us; the launch traced here: 228 us
  waiting for transfers between devices  100 us (44%)
  other arithmetic  68.7 us (30%)
  local copies, waits for them, and re-layouts  28.2 us (12%)
  between operations  17.4 us (8%)
  matrix products  9.46 us (4%)
  starting transfers between devices  4.56 us (2%)
    reduce_scatter x1, waiting for transfers between devices, on_device(): colours = lax.psum_scatter(terms, 'depth', scatter_dimension=3, tiled=True)  78.8 us
    reduce_sum x1, other arithmetic, march(): plain = jnp.sum(weight, axis=0)  31.7 us
    another operation x1, other arithmetic, march(): running = jnp.cumsum(optical, axis=0)  30.5 us
    all_gather x1, waiting for transfers between devices, on_device(): lax.all_gather(slab_tau[None], 'depth', axis=0, tiled=True)  21.2 us
    slice x2, local copies, waits for them, and re-layouts, centred(): lax.slice_in_dim(field, 1, size, axis=axis)  18.8 us
    dot_general x1, matrix products, on_device(): front_two = jnp.einsum('k,kxy->xy', later, tau_full, precision=HIGH)  4.8 us
    dot_general x1, matrix products, on_device(): front_one = jnp.einsum('k,kxy->xy', earlier, tau_full, precision=HIGH)  4.65 us
  transfers between devices with their start and end apart: 4, of which 2 were waited for; matrix products, arithmetic and copies ran while one was open for 24% of the time, Pallas kernels for 0%

commit v1 on v0

--- a/solution.py
+++ b/solution.py
@@ -76,7 +76,9 @@
     my_slab = slab_of[depth_place]
     earlier = (slab_of < my_slab).astype(jnp.float32)
     later = (slab_of > my_slab).astype(jnp.float32)
-    tau_full = lax.all_gather(slab_tau[None], "depth", axis=0, tiled=True).astype(jnp.float32)
+    tau_full = jnp.concatenate(
+        lax.all_to_all(jnp.stack([slab_tau[None]] * lax.axis_size("depth")), "depth", 0, 0), axis=0
+    ).astype(jnp.float32)
     front_one = jnp.einsum("k,kxy->xy", earlier, tau_full, precision=HIGH)
     front_two = jnp.einsum("k,kxy->xy", later, tau_full, precision=HIGH)
     total = jnp.sum(tau_full, axis=0)

time: 229 us -> 217 us (0.948)
  waiting for transfers between devices: 100 us -> 81.8 us
  starting transfers between devices: 4.56 us -> 12 us
  matrix products: 9.46 us -> 6 us
    all_gather x1 -> x0, waiting for transfers between devices: 21.2 us -> none  [on_device(): lax.all_gather(slab_tau[None], 'depth', axis=0, tiled=True)]
    all_to_all x0 -> x1, starting transfers between devices: none -> 7.48 us  [on_device(): lax.all_to_all(jnp.stack([slab_tau[None]] * lax.axis_size('depth')), 'dep...]
    reduce_scatter x1, waiting for transfers between devices: 78.8 us -> 81.8 us  [on_device(): colours = lax.psum_scatter(terms, 'depth', scatter_dimension=3, tiled=True)]
  transfers between devices with their start and end apart: 4 -> 4, of which waited for: 2 -> 1; matrix products, arithmetic and copies ran while one was open for 24% -> 26% of each run, Pallas kernels for 0% -> 0%
where the time goes in v1:
time: 217 us; the launch traced here: 216 us
  waiting for transfers between devices  81.8 us (38%)
  other arithmetic  69.2 us (32%)
  local copies, waits for them, and re-layouts  29.9 us (14%)
  between operations  17.5 us (8%)
  starting transfers between devices  12 us (6%)
  matrix products  6 us (3%)
    reduce_scatter x1, waiting for transfers between devices, on_device(): colours = lax.psum_scatter(terms, 'depth', scatter_dimension=3, tiled=True)  81.8 us
    reduce_sum x1, other arithmetic, march(): plain = jnp.sum(weight, axis=0)  32 us
    another operation x1, other arithmetic, march(): running = jnp.cumsum(optical, axis=0)  30.6 us
    slice x2, local copies, waits for them, and re-layouts, centred(): lax.slice_in_dim(field, 1, size, axis=axis)  18.9 us
    all_to_all x1, starting transfers between devices, on_device(): lax.all_to_all(jnp.stack([slab_tau[None]] * lax.axis_size('depth')), 'dep...  7.48 us
  transfers between devices with their start and end apart: 4, of which 1 were waited for; matrix products, arithmetic and copies ran while one was open for 26% of the time, Pallas kernels for 0%

profile of v1, /device:TPU:2, one launch (start us, length us, event | category | flops | bytes accessed | tf_op | source)
XLA Modules:
  0.0 216.4 jit_solution(13220744459441400342)
XLA Ops:
  6.5 2.7 %fusion.24 = (f32[32,1,2048]{2,1,0:T(1,128)S(1)}, f32[32,1,2048]{2,1,0:T(1,128)S(1)}) fusion(f32[32,32,2048]{2,1,0:T(8,128)} %param.4), kind=kLoop, calls=%fused_computation.47 | loop fusion | bytes 1048576 | tf_op jit(solution)/shard_map/slice | solution.py:69
  9.2 1.3 collective-permute-start
  10.5 3.0 %collective-permute-start.1 = (f32[32,1,2048]{2,1,0:T(1,128)S(1)}, f32[32,1,2048]{2,1,0:T(1,128)S(1)}, u32[]{:S(2)}, u32[]{:S(2)}) collective-permute-start(f32[32,1,2048]{2,1,0:T(1,128)S(1)} %get-tuple-element.20), channel_id=1, source_target_pairs={{0,1},{1,2},{2,3},{3,4},{4,5},{5,6},{6,7},{7,8},{8,9},{9,10},{10,1... | collective-permute-start | bytes 786440 | tf_op jit(solution)/shard_map/ppermute | solution.py:14
  13.6 1.2 fusion.23
  14.8 11.6 %fusion.22 = (f32[31,32,2048]{2,1,0:T(8,128)}, f32[31,32,2048]{2,1,0:T(8,128)}) fusion(f32[32,32,2048]{2,1,0:T(8,128)} %param.4), kind=kLoop, calls=%fused_computation.45 | loop fusion | bytes 32505856 | tf_op jit(solution)/shard_map/slice | solution.py:26
  26.5 7.3 %fusion.20 = (f32[32,32,2047]{2,1,0:T(8,128)}, f32[32,32,2047]{2,1,0:T(8,128)}) fusion(f32[32,32,2048]{2,1,0:T(8,128)S(1)} %bitcast.26), kind=kLoop, calls=%fused_computation.43 | loop fusion | bytes 33538048 | tf_op jit(solution)/shard_map/slice | solution.py:26
  33.7 0.7 fusion.25
  38.3 0.6 dynamic_slice.6
  39.0 1.4 fusion.21
  40.4 2.9 %broadcast_select_fusion.1 = (f32[32,1,2048]{2,1,0:T(1,128)S(1)}, f32[32,1,2048]{2,1,0:T(1,128)S(1)}) fusion(f32[32,1,2048]{2,1,0:T(1,128)S(1)} %collective-permute-done, pred[]{:T(512)S(6)} %eq.6, f32[32,32,2048]{2,1,0:T(8,128)} %param.4, f32[32,1,2048]{2,1,0:T(1,128)S(1)} %collective-permute-done.1, pred[]{:T(512)S(6)} %eq.7), kind=kLoop, calls=%fused_computation.25 | loop fusion | flops 131072 | bytes 1572866 | tf_op jit(solution)/shard_map/jit(_where)/select_n | solution.py:70
  43.3 30.6 %add_multiply_fusion.1 = (f32[32,32,2048]{2,1,0:T(8,128)}, f32[32,32,2048]{2,1,0:T(8,128)}) fusion(f32[32,32,2048]{2,1,0:T(8,128)} %param.4, f32[32,1,2048]{2,1,0:T(1,128)S(1)} %get-tuple-element.18, f32[32,1,2048]{2,1,0:T(1,128)S(1)} %get-tuple-element.17, f32[]{:T(128)} %bitcast.3, f32[]{:T(128)} %bitcast.2, f32[]{:T(128)} %bitcast.1, ...), kind=kOutput, calls=%fused_computation.8 | output fusion | flops 136314880 | bytes 59244556 | tf_op jit(solution)/shard_map/jit(cumsum)/reduce_window_sum | solution.py:44
  74.0 1.0 fusion.9
  74.9 1.7 slice_bitcast_fusion
  76.6 1.5 stack.19
  78.2 7.5 %all-to-all-start = ((bf16[16,1,32,2048]{3,2,1,0:T(8,128)(2,1)}), bf16[16,1,32,2048]{3,2,1,0:T(8,128)(2,1)S(1)}, u32[]{:S(2)}, u32[]{:S(2)}) async-start(bf16[16,1,32,2048]{3,2,1,0:T(8,128)(2,1)} %stack.19), calls=%async_computation | async-start | bytes 4194304 | tf_op jit(solution)/shard_map/all_to_all | solution.py:80
  85.6 0.2 reduce-scatter.2.cloned.1.call-start
  85.9 32.0 %fusion.19 = (f32[32,2048]{1,0:T(8,128)S(1)}, f32[32,2048]{1,0:T(8,128)S(1)}, f32[32,2048]{1,0:T(8,128)S(1)}, f32[32,2048]{1,0:T(8,128)S(1)}) fusion(f32[32,32,2048]{2,1,0:T(8,128)} %get-tuple-element.31, f32[32,32,2048]{2,1,0:T(8,128)} %param.4, f32[]{:T(128)} %bitcast.8, f32[31,32,2048]{2,1,0:T(8,128)} %get-tuple-element.14, f32[1,32,2048]{2,1,0:T(8,128)} %copy-done, ...), kind=kLoop, calls=%fused_computation.42 | loop fusion | flops 81526784 | bytes 60555276 | tf_op jit(solution)/shard_map/reduce_sum | solution.py:54
  117.9 0.3 add_convert_fusion.1
  118.2 3.0 %fusion.4 = f32[1,32,2048]{2,0,1:T(1,128)S(1)} fusion(bf16[16,32,2048]{2,1,0:T(8,128)(2,1)S(1)} %bitcast.27, s32[16]{0:T(128)S(1)} %copy-done.4, s32[]{:T(128)} %bitcast.9), kind=kOutput, calls=%fused_computation.15 | convolution fusion | flops 2097168 | bytes 2359364 | tf_op jit(solution)/shard_map/k,kxy->xy/dot_general | solution.py:83
  121.2 3.0 %fusion.6 = f32[1,32,2048]{2,0,1:T(1,128)S(1)} fusion(bf16[16,32,2048]{2,1,0:T(8,128)(2,1)S(1)} %bitcast.28, s32[16]{0:T(128)S(1)} %copy-done.4, s32[]{:T(128)} %bitcast.9), kind=kOutput, calls=%fused_computation.17 | convolution fusion | flops 2097168 | bytes 2359364 | tf_op jit(solution)/shard_map/k,kxy->xy/dot_general | solution.py:82
  124.5 1.3 convert_multiply_fusion
  125.8 0.4 convert_reduce_fusion
  126.2 81.8 %reduce-scatter.2.cloned.1.call-done = f32[2,3,32,128]{3,2,1,0:T(8,128)} async-done(((f32[2,3,32,2048]{3,2,1,0:T(8,128)}), f32[2,3,32,128]{3,2,1,0:T(8,128)}) %reduce-scatter.2.cloned.1.call-update) | async-done | bytes 98320 | tf_op jit(solution)/shard_map/reduce_scatter | solution.py:87
  208.0 1.6 pad_maximum_fusion.2
  (27 shorter events, 0.3 us)
Async XLA Ops:
  9.2 31.2 %collective-permute-start = (f32[32,1,2048]{2,1,0:T(1,128)S(1)}, f32[32,1,2048]{2,1,0:T(1,128)S(1)}, u32[]{:S(2)}, u32[]{:S(2)}) collective-permute-start(f32[32,1,2048]{2,1,0:T(1,128)S(1)} %get-tuple-element.19), channel_id=1, source_target_pairs={{1,0},{2,1},{3,2},{4,3},{5,4},{6,5},{7,6},{8,7},{9,8},{10,9},{11,1... | collective-permute-start | bytes 786440 | tf_op jit(solution)/shard_map/ppermute | solution.py:17
  10.5 29.9 %collective-permute-start.1 = (f32[32,1,2048]{2,1,0:T(1,128)S(1)}, f32[32,1,2048]{2,1,0:T(1,128)S(1)}, u32[]{:S(2)}, u32[]{:S(2)}) collective-permute-start(f32[32,1,2048]{2,1,0:T(1,128)S(1)} %get-tuple-element.20), channel_id=1, source_target_pairs={{0,1},{1,2},{2,3},{3,4},{4,5},{5,6},{6,7},{7,8},{8,9},{9,10},{10,1... | collective-permute-start | bytes 786440 | tf_op jit(solution)/shard_map/ppermute | solution.py:14
  13.6 12.8 %slice-start = ((s8[8388608]{0:T(1024)(128)(4,1)}), s8[4194304]{0:T(1024)(128)(4,1)S(1)}, s32[]{:S(2)}) async-start(s8[8388608]{0:T(1024)(128)(4,1)} %bitcast.25), calls=%async_computation.3 | async-start | bytes 8388608
  14.8 28.5 %copy-start = (f32[1,32,2048]{2,1,0:T(8,128)}, f32[1,32,2048]{2,1,0:T(8,128)S(1)}, u32[]{:S(2)}) copy-start(f32[1,32,2048]{2,1,0:T(8,128)S(1)} %get-tuple-element.16) | copy-start | bytes 786436
  14.8 11.6 %slice-start.1 = ((s8[8388608]{0:T(1024)(128)(4,1)}), s8[4194304]{0:T(1024)(128)(4,1)S(1)}, s32[]{:S(2)}) async-start(s8[8388608]{0:T(1024)(128)(4,1)} %bitcast.25), calls=%async_computation.4 | async-start | bytes 8388608
  26.4 7.3 %copy-start.5 = (f32[2,3]{1,0:T(2,128)S(1)}, f32[2,3]{1,0:T(2,128)}, u32[]{:S(2)}) copy-start(f32[2,3]{1,0:T(2,128)} %param.5) | copy-start | bytes 76
  26.4 7.3 %copy-start.3 = (f32[2,3]{1,0:T(2,128)S(1)}, f32[2,3]{1,0:T(2,128)}, u32[]{:S(2)}) copy-start(f32[2,3]{1,0:T(2,128)} %param.6) | copy-start | bytes 76
  26.4 11.9 %copy-start.4 = (s32[16]{0:T(128)S(1)}, s32[16]{0:T(128)}, u32[]{:S(2)}) copy-start(s32[16]{0:T(128)} %param.7) | copy-start | bytes 196
  43.3 30.7 %copy-start.1 = (f32[32,1,2048]{2,1,0:T(1,128)}, f32[32,1,2048]{2,1,0:T(1,128)S(1)}, u32[]{:S(2)}) copy-start(f32[32,1,2048]{2,1,0:T(1,128)S(1)} %get-tuple-element.17) | copy-start | bytes 786436
  43.3 30.7 %copy-start.2 = (f32[32,1,2048]{2,1,0:T(1,128)}, f32[32,1,2048]{2,1,0:T(1,128)S(1)}, u32[]{:S(2)}) copy-start(f32[32,1,2048]{2,1,0:T(1,128)S(1)} %get-tuple-element.18) | copy-start | bytes 786436
  78.2 40.0 %all-to-all-start = ((bf16[16,1,32,2048]{3,2,1,0:T(8,128)(2,1)}), bf16[16,1,32,2048]{3,2,1,0:T(8,128)(2,1)S(1)}, u32[]{:S(2)}, u32[]{:S(2)}) async-start(bf16[16,1,32,2048]{3,2,1,0:T(8,128)(2,1)} %stack.19), calls=%async_computation | async-start | bytes 4194304 | tf_op jit(solution)/shard_map/all_to_all | solution.py:80
  85.6 122.4 %reduce-scatter.2.cloned.1.call-start = ((), (), s32[]{:S(2)}) async-start(), calls=%async_computation.2 | async-start | bytes 1671168 | tf_op jit(solution)/shard_map/reduce_scatter | solution.py:87
Sparse Core Ops, SparseCore 0:
  125.9 82.0 reduce-scatter.1
